TPU v7x, 32 devices: a whole 2x2x4 slice. The times are simulated.
32 devices in a mesh: seq: 8 (over z, y), mp: 4 (over x, core).
Axes of the slice: x: 2, y: 2, z: 4, core: 2. Of those that a mesh axis runs over, the one named last changes fastest.
Arguments:
- incoming_image_patches: bfloat16 [1, 128, 128, 1152], P(None, 'seq', 'mp'), may hold values from -6 to 6
- initial_standardize_scaling: float32 [1152], replicated, may hold values from 0.1 to 1.9
- acceptance_matrix: bfloat16 [1152, 1024], P(None, 'mp'), may hold values from -0.1875 to 0.1875
- addressing_matrix: bfloat16 [1152, 1024], P(None, 'mp'), may hold values from -0.1875 to 0.1875
- content_matrix: bfloat16 [1152, 1024], P(None, 'mp'), may hold values from -0.1875 to 0.1875
- forgetting_lowdim_left_factor: bfloat16 [1152, 64], replicated, may hold values from -0.1875 to 0.1875
- forgetting_lowdim_right_factor: bfloat16 [64, 1024], P(None, 'mp'), may hold values from -1.5 to 1.5
- forgetting_baseline: float32 [1024], P('mp'), may hold values from -6 to 1
- self_token_reward: float32 [1024], P('mp'), may hold values from -3 to 3
- horizontal_cluster_scaling: float32 [1024], P('mp'), may hold values from 0.1 to 1.9
- vertical_cluster_scaling: float32 [1024], P('mp'), may hold values from 0.1 to 1.9
- temporal_mix_projection_matrix: bfloat16 [1024, 1152], P('mp'), may hold values from -0.1875 to 0.1875
- later_standardize_scaling: float32 [1152], replicated, may hold values from 0.1 to 1.9
- feature_mix_addressing_matrix: bfloat16 [1152, 4608], P('seq', 'mp'), may hold values from -0.1875 to 0.1875
- feature_mix_content_matrix: bfloat16 [4608, 1152], P('mp', 'seq'), may hold values from -0.09375 to 0.09375
Outputs:
- block_out: bfloat16 [1, 128, 128, 1152], P(None, 'seq', 'mp')
All inputs are finite; a program needn't handle non-finite values.
Results may differ from a plain program's by a relative error of at most 0.017.
Values may be sent and summed in bfloat16 or wider, within the bound.
A program may use at most 128 MiB of HBM per device.

v0:
```python
import jax
import jax.numpy as jnp
from jax import lax
from jax.sharding import PartitionSpec as P

SUBSPACE_SIZE = 64


def layer_norm(inputs, gain):
    values = inputs.astype(jnp.float32)
    average = jnp.mean(values, axis=-1, keepdims=True)
    centred = values - average
    spread = jnp.mean(centred * centred, axis=-1, keepdims=True)
    return (centred * lax.rsqrt(spread + 1e-05) * gain).astype(jnp.bfloat16)


def heads_first(array, nheads):
    number, length, inner_width = array.shape
    shaped = array.astype(jnp.float32).reshape(number, length, nheads, inner_width // nheads)
    return shaped.transpose(0, 2, 1, 3)


def recurrence(recept_in, keying_in, decays_in, valued_in, boost_in, gain):
    number, length, inner_width = recept_in.shape
    nheads = inner_width // SUBSPACE_SIZE
    head_size = inner_width // nheads
    blocks = length // 16
    acceptance_horizontal_lines = heads_first(recept_in, nheads)
    addressing_horizontal_lines = heads_first(keying_in, nheads)
    decays = heads_first(decays_in, nheads)
    content_horizontal_lines = heads_first(valued_in, nheads)
    boost = boost_in.reshape(nheads, 1, head_size)
    running = jnp.cumsum(decays, axis=2)
    before = running - decays
    before_blocks = before.reshape(number, nheads, blocks, 16, head_size)
    anchor = before_blocks[:, :, :, :1, :]
    queries = acceptance_horizontal_lines.reshape(number, nheads, blocks, 16, head_size) * jnp.exp(
        before_blocks - anchor
    )
    places = jnp.arange(length)
    limits = (jnp.arange(blocks) + 1) * 16
    usable = places[None, :] < limits[:, None]
    exponent = anchor - running[:, :, None, :, :]
    exponent = jnp.where(usable[None, None, :, :, None], exponent, -10000.0)
    weighted = addressing_horizontal_lines[:, :, None, :, :] * jnp.exp(exponent)
    scores = jnp.einsum("nhbqc,nhbsc->nhbqs", queries, weighted, precision=lax.Precision.HIGHEST)
    query_places = places.reshape(blocks, 16)
    earlier = places[None, None, :] < query_places[:, :, None]
    scores = jnp.where(earlier[None, None], scores, 0.0)
    current = jnp.sum(acceptance_horizontal_lines * boost * addressing_horizontal_lines, axis=-1)
    summed = jnp.einsum(
        "nhbqs,nhsc->nhbqc", scores, content_horizontal_lines, precision=lax.Precision.HIGHEST
    )
    summed = (
        summed.reshape(number, nheads, length, head_size)
        + current[..., None] * content_horizontal_lines
    )
    average = jnp.mean(summed, axis=-1, keepdims=True)
    centred = summed - average
    spread = jnp.mean(centred * centred, axis=-1, keepdims=True)
    normed = (
        (centred * lax.rsqrt(spread + 0.00064))
        .transpose(0, 2, 1, 3)
        .reshape(number, length, inner_width)
    )
    return (normed * gain).astype(jnp.bfloat16)


def lines_of_columns(array):
    images, height, columns, inner_width = array.shape
    return jnp.swapaxes(array, 1, 2).reshape(images * columns, height, inner_width)


def shards(
    incoming_image_patches,
    initial_standardize_scaling,
    acceptance_matrix,
    addressing_matrix,
    content_matrix,
    forgetting_lowdim_left_factor,
    forgetting_lowdim_right_factor,
    forgetting_baseline,
    self_token_reward,
    horizontal_cluster_scaling,
    vertical_cluster_scaling,
    temporal_mix_projection_matrix,
    later_standardize_scaling,
    feature_mix_addressing_matrix,
    feature_mix_content_matrix,
):
    images, row_count, part_cols, model_width = incoming_image_patches.shape
    whole_rows = lax.all_gather(incoming_image_patches, "mp", axis=2, tiled=True)
    full_cols = whole_rows.shape[2]
    inner_width = acceptance_matrix.shape[1]
    grid_shape = (images, row_count, full_cols, inner_width)
    xn1 = layer_norm(whole_rows, initial_standardize_scaling).reshape(-1, model_width)
    acceptance_horizontal_lines = jnp.dot(
        xn1, acceptance_matrix, preferred_element_type=jnp.float32
    ).astype(jnp.bfloat16)
    addressing_horizontal_lines = jnp.dot(
        xn1, addressing_matrix, preferred_element_type=jnp.float32
    ).astype(jnp.bfloat16)
    content_horizontal_lines = jnp.dot(
        xn1, content_matrix, preferred_element_type=jnp.float32
    ).astype(jnp.bfloat16)
    latent = jnp.tanh(
        jnp.dot(xn1, forgetting_lowdim_left_factor, preferred_element_type=jnp.float32)
    ).astype(jnp.bfloat16)
    forgetting_log_amount = (
        -0.7
        * jax.nn.sigmoid(
            forgetting_baseline
            + jnp.dot(latent, forgetting_lowdim_right_factor, preferred_element_type=jnp.float32)
        )
    ).astype(jnp.bfloat16)
    recept_grid = acceptance_horizontal_lines.reshape(grid_shape)
    keying_grid = addressing_horizontal_lines.reshape(grid_shape)
    decay_grid = forgetting_log_amount.reshape(grid_shape)
    line_shape = (images * row_count, full_cols, inner_width)
    horizontal_recurrence_result = recurrence(
        acceptance_horizontal_lines.reshape(line_shape),
        addressing_horizontal_lines.reshape(line_shape),
        forgetting_log_amount.reshape(line_shape),
        content_horizontal_lines.reshape(line_shape),
        self_token_reward,
        horizontal_cluster_scaling,
    )
    col_recept, col_keying, col_decay, col_valued = (
        lax.all_to_all(recept_grid, "seq", split_axis=2, concat_axis=1, tiled=True),
        lax.all_to_all(keying_grid, "seq", split_axis=2, concat_axis=1, tiled=True),
        lax.all_to_all(decay_grid, "seq", split_axis=2, concat_axis=1, tiled=True),
        lax.all_to_all(
            horizontal_recurrence_result.reshape(grid_shape),
            "seq",
            split_axis=2,
            concat_axis=1,
            tiled=True,
        ),
    )
    height = col_recept.shape[1]
    columns = col_recept.shape[2]
    vertical_recurrence_result = recurrence(
        lines_of_columns(col_recept),
        lines_of_columns(col_keying),
        lines_of_columns(col_decay),
        lines_of_columns(col_valued),
        self_token_reward,
        vertical_cluster_scaling,
    )
    back_grid = jnp.swapaxes(
        vertical_recurrence_result.reshape(images, columns, height, inner_width), 1, 2
    )
    row_grid = lax.all_to_all(back_grid, "seq", split_axis=1, concat_axis=2, tiled=True)
    partial_value = jnp.dot(
        row_grid.reshape(-1, inner_width),
        temporal_mix_projection_matrix,
        preferred_element_type=jnp.float32,
    )
    partial_value = lax.optimization_barrier(partial_value.astype(jnp.bfloat16)).astype(jnp.float32)
    partial_value = partial_value.reshape(images, row_count, full_cols, model_width)
    totals = lax.psum(partial_value.astype(jnp.bfloat16), "mp").astype(jnp.float32)
    residual_all = (whole_rows.astype(jnp.float32) + totals).astype(jnp.bfloat16)
    mix_input = layer_norm(residual_all, later_standardize_scaling)
    residual = lax.dynamic_slice_in_dim(
        residual_all, lax.axis_index("mp") * part_cols, part_cols, 2
    )
    flattened = mix_input.reshape(-1, model_width)
    hidden_pre = jnp.dot(
        flattened,
        lax.all_gather(feature_mix_addressing_matrix, "seq", axis=0, tiled=True),
        preferred_element_type=jnp.float32,
    )
    positive = jnp.maximum(hidden_pre, 0.0)
    hidden = (positive * positive).astype(jnp.bfloat16)
    downward = jnp.dot(
        hidden,
        lax.all_gather(feature_mix_content_matrix, "seq", axis=1, tiled=True),
        preferred_element_type=jnp.float32,
    )
    downward = lax.optimization_barrier(downward.astype(jnp.bfloat16)).astype(jnp.float32)
    downward = downward.reshape(images, row_count, full_cols, model_width)
    mixed = lax.psum_scatter(
        downward.astype(jnp.bfloat16), "mp", scatter_dimension=2, tiled=True
    ).astype(jnp.float32)
    return (residual.astype(jnp.float32) + mixed).astype(jnp.bfloat16)


def solution(mesh):
    placed = (
        P(None, "seq", "mp", None),
        P(),
        P(None, "mp"),
        P(None, "mp"),
        P(None, "mp"),
        P(),
        P(None, "mp"),
        P("mp"),
        P("mp"),
        P("mp"),
        P("mp"),
        P("mp", None),
        P(),
        P("seq", "mp"),
        P("mp", "seq"),
    )
    return jax.shard_map(
        shards, mesh=mesh, in_specs=placed, out_specs=P(None, "seq", "mp", None), check_vma=False
    )
```

profile of v0, /device:TPU:0, one launch (start us, length us, event | category | flops | bytes accessed | tf_op | source)
XLA Modules:
  0.0 550.7 jit_solution(13070111403937969308)
XLA Ops:
  9.0 40.9 %all-gather.4.cloned.1.call-done = bf16[1,16,128,1152]{3,2,1,0:T(8,128)(2,1)} async-done(((bf16[1,16,32,1152]{3,2,1,0:T(8,128)(2,1)}), bf16[1,16,128,1152]{3,2,1,0:T(8,128)(2,1)}) %all-gather.4.cloned.1.call-update) | async-done | bytes 4718608 | tf_op jit(solution)/shard_map/all_gather | solution.py:92
  49.9 3.2 convert_reduce_fusion
  55.1 1.9 fusion.18
  57.0 2.2 copy-done.9
  59.2 1.6 convolution_convert_fusion.4
  60.8 3.1 reshape.301
  63.9 4.9 copy.216
  68.8 4.8 copy.187
  73.7 4.5 fusion.54
  78.1 3.1 reshape.302
  81.3 8.0 %bitcast_subtract_fusion = (f32[16,4,128,64]{3,0,1,2:T(8,128)S(1)}, f32[16,4,128,64]{3,0,1,2:T(8,128)}) fusion(f32[16,128,4,64]{3,2,1,0:T(4,128)} %reshape.302), kind=kOutput, calls=%fused_computation.42 | output fusion | flops 67108864 | bytes 6291456 | tf_op jit(solution)/shard_map/jit(cumsum)/reduce_window_sum | solution.py:33
  89.3 1.9 copy-done.8
  91.4 4.8 copy.196
  96.2 3.9 convolution_convert_fusion.3
  101.1 3.7 reshape.303
  104.8 3.5 copy.194
  108.3 5.7 %convolution_convert_fusion.2 = bf16[2048,256]{1,0:T(8,128)(2,1)} fusion(bf16[2048,1152]{1,0:T(8,128)(2,1)} %bitcast.152, bf16[1152,256]{1,0:T(8,128)(2,1)} %param.19), kind=kOutput, calls=%fused_computation.66 | convolution fusion | flops 1208483840 | bytes 6356992 | tf_op jit(solution)/shard_map/dot_general | solution.py:103
  114.1 2.3 copy.197
  117.8 22.1 %fusion.1 = f32[16,4,8,16,128]{4,3,2,1,0:T(8,128)S(1)} fusion(f32[16,4,128,64]{2,3,1,0:T(8,128)} %copy.196, f32[16,4,8,64]{3,2,1,0:T(8,128)S(1)} %copy.191, f32[16,4,128,64]{2,3,1,0:T(8,128)S(1)} %bitcast.135, pred[8,128]{1,0:T(8,128)(4,1)S(1)} %iota_compare_fusion.1, f32[16,4,8,16,64]{4,3,2,1,0:T(8,128)} %bitcast.161, f32[16,4,8,16,64]{4,0,1,3,2:T(8,128)} %bitcast.147), kind=kOutput, calls=%fused_computation.1 | convolution fusion | flops 818937856 | bytes 12715008 | tf_op jit(solution)/shard_map/nhbqc,nhbsc->nhbqs/dot_general | solution.py:46
  140.0 3.9 fusion.44
  143.8 3.2 copy.200
  147.1 2.9 fusion.57
  150.9 1.8 subtract_multiply_fusion.1
  152.7 2.3 copy.201
  156.3 5.6 %all-to-all-start.3 = ((bf16[1,16,128,256]{3,1,0,2:T(8,128)(2,1)}), bf16[1,16,128,256]{3,1,0,2:T(8,128)(2,1)}, u32[]{:S(2)}, u32[]{:S(2)}) async-start(bf16[1,16,128,256]{3,1,0,2:T(8,128)(2,1)} %multiply_convert_fusion.1), calls=%async_computation.3 | async-start | bytes 2097152 | tf_op jit(solution)/shard_map/all_to_all | solution.py:132
  162.0 2.9 copy.173
  164.8 23.4 %all-to-all-done.3 = bf16[1,16,128,256]{3,1,0,2:T(8,128)(2,1)} async-done(((bf16[1,16,128,256]{3,1,0,2:T(8,128)(2,1)}), bf16[1,16,128,256]{3,1,0,2:T(8,128)(2,1)}, u32[]{:S(2)}, u32[]{:S(2)}) %all-to-all-start.3) | async-done | bytes 1048608 | tf_op jit(solution)/shard_map/all_to_all | solution.py:132
  188.2 4.2 all-to-all-start.1
  192.5 1.6 copy.168
  194.0 24.0 %all-to-all-done.1 = bf16[1,16,128,256]{3,1,0,2:T(8,128)(2,1)} async-done(((bf16[1,16,128,256]{3,1,0,2:T(8,128)(2,1)}), bf16[1,16,128,256]{3,1,0,2:T(8,128)(2,1)}, u32[]{:S(2)}, u32[]{:S(2)}) %all-to-all-start.1) | async-done | bytes 1048608 | tf_op jit(solution)/shard_map/all_to_all | solution.py:131
  218.1 3.6 all-to-all-start
  221.6 1.6 copy.180
  223.2 24.2 %all-to-all-done = bf16[1,16,128,256]{3,1,0,2:T(8,128)(2,1)S(1)} async-done(((bf16[1,16,128,256]{3,1,0,2:T(8,128)(2,1)}), bf16[1,16,128,256]{3,1,0,2:T(8,128)(2,1)S(1)}, u32[]{:S(2)}, u32[]{:S(2)}) %all-to-all-start) | async-done | bytes 1048608 | tf_op jit(solution)/shard_map/all_to_all | solution.py:129
  247.5 4.2 all-to-all-start.2
  251.8 1.6 copy.202
  253.4 1.7 copy.204
  255.1 1.6 copy.174
  257.0 1.6 copy.175
  258.6 2.0 copy.176
  260.5 4.6 copy.177
  265.1 6.1 %bitcast_subtract_fusion.1 = (f32[16,4,128,64]{3,0,1,2:T(8,128)S(1)}, f32[16,4,128,64]{3,0,1,2:T(8,128)}) fusion(f32[16,128,4,64]{3,0,2,1:T(8,128)} %copy.177), kind=kOutput, calls=%fused_computation.45 | output fusion | flops 67108864 | bytes 6291456 | tf_op jit(solution)/shard_map/jit(cumsum)/reduce_window_sum | solution.py:33
  271.2 2.0 copy-done.7
  273.4 4.7 copy.185
  278.8 1.5 copy.170
  280.3 2.0 copy.171
  282.3 2.8 copy.172
  285.1 1.6 copy.181
  287.0 1.5 copy.182
  288.5 3.0 copy.183
  291.5 22.4 %fusion.6 = f32[16,4,8,16,128]{4,3,2,1,0:T(8,128)S(1)} fusion(f32[16,4,128,64]{2,3,1,0:T(8,128)} %copy.185, f32[16,4,8,64]{3,2,1,0:T(8,128)S(1)} %copy.178, f32[16,4,128,64]{2,3,1,0:T(8,128)} %bitcast.140, pred[8,128]{1,0:T(8,128)(4,1)S(1)} %iota_compare_fusion.1, f32[16,4,8,16,64]{4,3,2,1,0:T(8,128)} %bitcast.160, f32[16,4,8,16,64]{4,0,1,3,2:T(8,128)} %bitcast.145), kind=kOutput, calls=%fused_computation.6 | convolution fusion | flops 818937856 | bytes 12715008 | tf_op jit(solution)/shard_map/nhbqc,nhbsc->nhbqs/dot_general | solution.py:46
  313.8 3.8 fusion.46
  317.6 4.2 copy.205
  321.8 3.2 fusion.80
  326.0 2.1 copy.210
  328.1 1.9 fusion.68
  330.0 30.6 %all_to_all.69 = bf16[1,128,16,256]{3,2,0,1:T(8,128)(2,1)S(1)} all-to-all(bf16[1,128,16,256]{3,2,0,1:T(8,128)(2,1)S(1)} %fusion.68), channel_id=1, replica_groups=mesh['seq'=8,'mp'=4] {'seq'}, dimensions={1} | all-to-all | bytes 2097152 | tf_op jit(solution)/shard_map/all_to_all | solution.py:153
  360.7 3.7 convolution_convert_fusion.1
  365.7 91.0 %all-reduce.2.cloned.1.call-done = bf16[1,16,128,1152]{3,2,1,0:T(8,128)(2,1)} async-done(((bf16[1,16,128,1152]{3,2,1,0:T(8,128)(2,1)}), bf16[1,16,128,1152]{3,2,1,0:T(8,128)(2,1)}) %all-reduce.2.cloned.1.call-update) | async-done | bytes 4718608 | tf_op jit(solution)/shard_map/psum | solution.py:161
  456.6 5.3 convert_reduce_fusion.1
  464.0 3.2 fusion.21
  467.3 8.3 %all-gather.8.cloned.1.call-done = bf16[1152,1152]{0,1:T(8,128)(2,1)} async-done(((bf16[1152,144]{0,1:T(8,128)(2,1)}), bf16[1152,1152]{0,1:T(8,128)(2,1)}) %all-gather.8.cloned.1.call-update) | async-done | bytes 2654224 | tf_op jit(solution)/shard_map/all_gather | solution.py:177
  475.5 18.4 %convolution_convert_fusion = bf16[2048,1152]{1,0:T(8,128)(2,1)} fusion(bf16[1152,1152]{0,1:T(8,128)(2,1)} %all-gather.8.cloned.1.call-done, bf16[2048,1152]{1,0:T(8,128)(2,1)} %bitcast.153, bf16[1152,1152]{1,0:T(8,128)(2,1)} %all-gather.6.cloned.1.call-done), kind=kOutput, calls=%fused_computation.40 | convolution fusion | flops 10881073152 | bytes 14745600 | tf_op jit(solution)/shard_map/dot_general | solution.py:175
  493.9 46.6 %reduce-scatter.2.cloned.1.call-done = bf16[1,16,32,1152]{3,2,1,0:T(8,128)(2,1)} async-done(((bf16[1,16,128,1152]{3,2,1,0:T(8,128)(2,1)}), bf16[1,16,32,1152]{3,2,1,0:T(8,128)(2,1)}) %reduce-scatter.2.cloned.1.call-update) | async-done | bytes 1179664 | tf_op jit(solution)/shard_map/reduce_scatter | solution.py:182
  540.5 2.9 add_convert_fusion
  (95 shorter events, 14.3 us)
Async XLA Ops:
  7.4 353.3 %copy-start = (bf16[256,1152]{1,0:T(8,128)(2,1)S(1)}, bf16[256,1152]{1,0:T(8,128)(2,1)}, u32[]{:S(2)}) copy-start(bf16[256,1152]{1,0:T(8,128)(2,1)} %param.26) | copy-start | bytes 1769476
  7.4 42.5 %all-gather.4.cloned.1.call-start = ((), (), s32[]{:S(2)}) async-start(), calls=%async_computation.6 | async-start | bytes 5898240 | tf_op jit(solution)/shard_map/all_gather | solution.py:92
  9.0 46.1 %copy-start.17 = (f32[1152]{0:T(1024)S(1)}, f32[1152]{0:T(1024)}, u32[]{:S(2)}) copy-start(f32[1152]{0:T(1024)} %param.16) | copy-start | bytes 13828
  49.9 3.8 copy-start.1
  55.1 4.1 copy-start.21
  57.0 2.2 copy-start.9
  60.8 8.0 %copy-start.10 = (bf16[2048,256]{1,0:T(8,128)(2,1)}, bf16[2048,256]{1,0:T(8,128)(2,1)S(1)}, u32[]{:S(2)}) copy-start(bf16[2048,256]{1,0:T(8,128)(2,1)S(1)} %convolution_convert_fusion.4) | copy-start | bytes 3145732
  68.8 4.8 copy-start.23
  68.8 4.8 copy-start.24
  68.8 4.8 copy-start.25
  78.1 11.1 %copy-start.14 = (bf16[2048,256]{1,0:T(8,128)(2,1)}, bf16[2048,256]{1,0:T(8,128)(2,1)S(1)}, u32[]{:S(2)}) copy-start(bf16[2048,256]{1,0:T(8,128)(2,1)S(1)} %fusion.54) | copy-start | bytes 3145732
  89.3 1.9 copy-start.8
  89.3 7.0 %copy-start.22 = (bf16[1152,256]{1,0:T(8,128)(2,1)S(1)}, bf16[1152,256]{1,0:T(8,128)(2,1)}, u32[]{:S(2)}) copy-start(bf16[1152,256]{1,0:T(8,128)(2,1)} %param.18) | copy-start | bytes 1769476
  100.1 1.0 copy-start.12
  108.3 9.5 %copy-start.6 = (f32[16,128,4,64]{1,3,2,0:T(8,128)}, f32[16,128,4,64]{1,3,2,0:T(8,128)S(1)}, u32[]{:S(2)}) copy-start(f32[16,128,4,64]{1,3,2,0:T(8,128)S(1)} %copy.194) | copy-start | bytes 6291460
  117.8 22.1 %copy-start.3 = (bf16[32,8,16,128]{3,2,1,0:T(8,128)(2,1)}, bf16[32,8,16,128]{3,2,1,0:T(8,128)(2,1)S(1)}, u32[]{:S(2)}) copy-start(bf16[32,8,16,128]{3,2,1,0:T(8,128)(2,1)S(1)} %copy.223) | copy-start | bytes 3145732
  147.1 2.9 copy-start.4
  150.9 4.2 copy-start.19
  156.3 36.2 %copy-start.11 = (bf16[2048,256]{1,0:T(8,128)(2,1)S(1)}, bf16[2048,256]{1,0:T(8,128)(2,1)}, u32[]{:S(2)}) copy-start(bf16[2048,256]{1,0:T(8,128)(2,1)} %copy-done.10) | copy-start | bytes 3145732
  156.3 31.9 %all-to-all-start.3 = ((bf16[1,16,128,256]{3,1,0,2:T(8,128)(2,1)}), bf16[1,16,128,256]{3,1,0,2:T(8,128)(2,1)}, u32[]{:S(2)}, u32[]{:S(2)}) async-start(bf16[1,16,128,256]{3,1,0,2:T(8,128)(2,1)} %multiply_convert_fusion.1), calls=%async_computation.3 | async-start | bytes 2097152 | tf_op jit(solution)/shard_map/all_to_all | solution.py:132
  161.9 59.7 %copy-start.13 = (bf16[2048,256]{1,0:T(8,128)(2,1)S(1)}, bf16[2048,256]{1,0:T(8,128)(2,1)}, u32[]{:S(2)}) copy-start(bf16[2048,256]{1,0:T(8,128)(2,1)} %copy-done.12) | copy-start | bytes 3145732
  188.2 29.8 %all-to-all-start.1 = ((bf16[1,16,128,256]{3,1,0,2:T(8,128)(2,1)}), bf16[1,16,128,256]{3,1,0,2:T(8,128)(2,1)}, u32[]{:S(2)}, u32[]{:S(2)}) async-start(bf16[1,16,128,256]{3,1,0,2:T(8,128)(2,1)} %copy.173), calls=%async_computation.1 | async-start | bytes 2097152 | tf_op jit(solution)/shard_map/all_to_all | solution.py:131
  218.1 29.4 %all-to-all-start = ((bf16[1,16,128,256]{3,1,0,2:T(8,128)(2,1)}), bf16[1,16,128,256]{3,1,0,2:T(8,128)(2,1)S(1)}, u32[]{:S(2)}, u32[]{:S(2)}) async-start(bf16[1,16,128,256]{3,1,0,2:T(8,128)(2,1)} %copy.168), calls=%async_computation | async-start | bytes 2097152 | tf_op jit(solution)/shard_map/all_to_all | solution.py:129
  247.5 7.7 %copy-start.15 = (bf16[1,16,128,256]{3,1,0,2:T(8,128)(2,1)}, bf16[1,16,128,256]{3,1,0,2:T(8,128)(2,1)S(1)}, u32[]{:S(2)}) copy-start(bf16[1,16,128,256]{3,1,0,2:T(8,128)(2,1)S(1)} %all-to-all-done) | copy-start | bytes 3145732
  247.5 37.7 %all-to-all-start.2 = ((bf16[1,16,128,256]{3,1,0,2:T(8,128)(2,1)}), bf16[1,16,128,256]{3,1,0,2:T(8,128)(2,1)}, u32[]{:S(2)}, u32[]{:S(2)}) async-start(bf16[1,16,128,256]{3,1,0,2:T(8,128)(2,1)} %copy.180), calls=%async_computation.2 | async-start | bytes 2097152 | tf_op jit(solution)/shard_map/all_to_all | solution.py:130
  251.7 204.9 %all-reduce.2.cloned.1.call-start = ((), (), s32[]{:S(2)}) async-start(), calls=%async_computation.7 | async-start | bytes 9437184 | tf_op jit(solution)/shard_map/psum | solution.py:161
  271.2 2.0 copy-start.7
  271.2 7.0 %copy-start.16 = (bf16[1,16,128,256]{3,1,0,2:T(8,128)(2,1)S(1)}, bf16[1,16,128,256]{3,1,0,2:T(8,128)(2,1)}, u32[]{:S(2)}) copy-start(bf16[1,16,128,256]{3,1,0,2:T(8,128)(2,1)} %copy-done.15) | copy-start | bytes 3145732
  291.5 22.4 %copy-start.5 = (bf16[1,16,128,256]{2,3,1,0:T(8,128)(2,1)S(1)}, bf16[1,16,128,256]{2,3,1,0:T(8,128)(2,1)}, u32[]{:S(2)}) copy-start(bf16[1,16,128,256]{2,3,1,0:T(8,128)(2,1)} %copy.204) | copy-start | bytes 3145732
  325.5 2.6 copy-start.20
  364.4 102.8 %all-gather.6.cloned.1.call-start = ((), (), s32[]{:S(2)}) async-start(), calls=%async_computation.8 | async-start | bytes 2985984 | tf_op jit(solution)/shard_map/all_gather | solution.py:170
  365.0 110.5 %all-gather.8.cloned.1.call-start = ((), (), s32[]{:S(2)}) async-start(), calls=%async_computation.9 | async-start | bytes 2985984 | tf_op jit(solution)/shard_map/all_gather | solution.py:177
  365.6 174.9 %reduce-scatter.2.cloned.1.call-start = ((), (), s32[]{:S(2)}) async-start(), calls=%async_computation.10 | async-start | bytes 5898240 | tf_op jit(solution)/shard_map/reduce_scatter | solution.py:182
  461.9 2.1 copy-start.2
  461.9 2.1 copy-start.18
Sparse Core Ops, SparseCore 0:
  9.7 40.1 all-gather.3
  364.6 92.0 all-reduce.1
  494.0 46.4 reduce-scatter.1
Sparse Core Ops, SparseCore 1:
  367.1 52.9 all-gather.5
  422.1 53.4 all-gather.7
where the time goes:
time: 554 us; the launch traced here: 551 us
  waiting for transfers between devices  260 us (47%)
  local copies, waits for them, and re-layouts  89.8 us (16%)
  matrix products  89.8 us (16%)
  other arithmetic  47.2 us (9%)
  blocking collectives  30.6 us (6%)
  starting transfers between devices  17.9 us (3%)
  between operations  15.3 us (3%)
    psum x1, waiting for transfers between devices, shards(): lax.psum(partial_value.astype(jnp.bfloat16), 'mp').astype(jnp.float32)  91 us
    reduce_scatter x1, waiting for transfers between devices, shards(): lax.psum_scatter(downward.astype(jnp.bfloat16), 'mp', scatter_dimension=2...  46.6 us
    dot_general x2, matrix products, recurrence(): jnp.einsum('nhbqc,nhbsc->nhbqs', queries, weighted, precision=lax.Precisi...  44.5 us
    transpose x14, local copies, waits for them, and re-layouts, heads_first(): return shaped.transpose(0, 2, 1, 3)  42.1 us
    all_gather x1, waiting for transfers between devices, shards(): lax.all_gather(incoming_image_patches, 'mp', axis=2, tiled=True)  40.9 us
    all_to_all x1, blocking collectives, shards(): lax.all_to_all(back_grid, 'seq', split_axis=1, concat_axis=2, tiled=True)  30.6 us
    all_to_all x1, waiting for transfers between devices, shards(): lax.all_to_all(recept_grid, 'seq', split_axis=2, concat_axis=1, tiled=True)  24.2 us
    all_to_all x1, waiting for transfers between devices, shards(): lax.all_to_all(decay_grid, 'seq', split_axis=2, concat_axis=1, tiled=True)  24 us
  transfers between devices with their start and end apart: 9, of which 7 were waited for; matrix products, arithmetic and copies ran while one was open for 9% of the time, Pallas kernels for 0%

commit v1 on v0

--- a/solution.py
+++ b/solution.py
@@ -89,7 +89,14 @@
     feature_mix_content_matrix,
 ):
     images, row_count, part_cols, model_width = incoming_image_patches.shape
-    whole_rows = lax.all_gather(incoming_image_patches, "mp", axis=2, tiled=True)
+    size = lax.axis_size("mp")
+    right = [(i, (i + 1) % size) for i in range(size)]
+    shards_2 = [incoming_image_patches]
+    for reach in range(1, size):
+        shards_2 = [lax.ppermute(shards_2[0], "mp", right), *shards_2]
+    out = jnp.concatenate(shards_2, axis=2)
+    turn = (lax.axis_index("mp") + 1) * shards_2[-1].shape[2]
+    whole_rows = jnp.roll(out, turn, axis=2)
     full_cols = whole_rows.shape[2]
     inner_width = acceptance_matrix.shape[1]
     grid_shape = (images, row_count, full_cols, inner_width)

time: 554 us -> 564 us (1.018)
    ppermute x0 -> x3, waiting for transfers between devices: none -> 46.8 us  [shards(): shards_2 = [lax.ppermute(shards_2[0], 'mp', right), *shards_2]]
    all_gather x1 -> x0, waiting for transfers between devices: 40.9 us -> none  [shards(): lax.all_gather(incoming_image_patches, 'mp', axis=2, tiled=True)]
    all_to_all x1, waiting for transfers between devices: 24.2 us -> 0.01 us  [shards(): lax.all_to_all(recept_grid, 'seq', split_axis=2, concat_axis=1, tiled=True)]
    all_to_all x1, waiting for transfers between devices: 0.01 us -> 24.2 us  [shards(): lax.all_to_all(keying_grid, 'seq', split_axis=2, concat_axis=1, tiled=True)]
    all_gather x1, waiting for transfers between devices: 8.25 us -> 0.01 us  [shards(): lax.all_gather(feature_mix_content_matrix, 'seq', axis=1, tiled=True)]
    all_gather x1, waiting for transfers between devices: 0.01 us -> 8.25 us  [shards(): lax.all_gather(feature_mix_addressing_matrix, 'seq', axis=0, tiled=True)]
    unnamed x53 -> x58, local copies, waits for them, and re-layouts: 9.93 us -> 13.2 us
  transfers between devices with their start and end apart: 9 -> 11, of which waited for: 7 -> 9; matrix products, arithmetic and copies ran while one was open for 9% -> 8% of each run, Pallas kernels for 0% -> 0%
where the time goes in v1:
time: 564 us; the launch traced here: 559 us
  waiting for transfers between devices  264 us (47%)
  local copies, waits for them, and re-layouts  91.8 us (16%)
  matrix products  90.1 us (16%)
  other arithmetic  47.4 us (8%)
  blocking collectives  30.6 us (5%)
  starting transfers between devices  19.5 us (3%)
  between operations  15.7 us (3%)
    psum x1, waiting for transfers between devices, shards(): lax.psum(partial_value.astype(jnp.bfloat16), 'mp').astype(jnp.float32)  91 us
    ppermute x3, waiting for transfers between devices, shards(): shards_2 = [lax.ppermute(shards_2[0], 'mp', right), *shards_2]  46.8 us
    reduce_scatter x1, waiting for transfers between devices, shards(): lax.psum_scatter(downward.astype(jnp.bfloat16), 'mp', scatter_dimension=2...  46.6 us
    dot_general x2, matrix products, recurrence(): jnp.einsum('nhbqc,nhbsc->nhbqs', queries, weighted, precision=lax.Precisi...  44.7 us
    transpose x14, local copies, waits for them, and re-layouts, heads_first(): return shaped.transpose(0, 2, 1, 3)  38.8 us
    all_to_all x1, blocking collectives, shards(): lax.all_to_all(back_grid, 'seq', split_axis=1, concat_axis=2, tiled=True)  30.6 us
    all_to_all x1, waiting for transfers between devices, shards(): lax.all_to_all(keying_grid, 'seq', split_axis=2, concat_axis=1, tiled=True)  24.2 us
    all_to_all x1, waiting for transfers between devices, shards(): lax.all_to_all(decay_grid, 'seq', split_axis=2, concat_axis=1, tiled=True)  23.8 us
  transfers between devices with their start and end apart: 11, of which 9 were waited for; matrix products, arithmetic and copies ran while one was open for 8% of the time, Pallas kernels for 0%

profile of v1, /device:TPU:0, one launch (start us, length us, event | category | flops | bytes accessed | tf_op | source)
XLA Modules:
  0.0 559.2 jit_solution(9488123631591031810)
XLA Ops:
  7.9 16.0 %collective-permute-done = bf16[1,16,32,1152]{3,2,1,0:T(8,128)(2,1)S(1)} collective-permute-done((bf16[1,16,32,1152]{3,2,1,0:T(8,128)(2,1)}, bf16[1,16,32,1152]{3,2,1,0:T(8,128)(2,1)S(1)}, u32[]{:S(2)}, u32[]{:S(2)}) %collective-permute-start) | collective-permute-done | bytes 1179680 | tf_op jit(solution)/shard_map/ppermute | solution.py:96
  23.9 15.7 %collective-permute-done.1 = bf16[1,16,32,1152]{3,2,1,0:T(8,128)(2,1)} collective-permute-done((bf16[1,16,32,1152]{3,2,1,0:T(8,128)(2,1)S(1)}, bf16[1,16,32,1152]{3,2,1,0:T(8,128)(2,1)}, u32[]{:S(2)}, u32[]{:S(2)}) %collective-permute-start.1) | collective-permute-done | bytes 1179680 | tf_op jit(solution)/shard_map/ppermute | solution.py:96
  40.6 15.0 %collective-permute-done.2 = bf16[1,16,32,1152]{3,2,1,0:T(8,128)(2,1)} collective-permute-done((bf16[1,16,32,1152]{3,2,1,0:T(8,128)(2,1)}, bf16[1,16,32,1152]{3,2,1,0:T(8,128)(2,1)}, u32[]{:S(2)}, u32[]{:S(2)}) %collective-permute-start.2) | collective-permute-done | bytes 1179680 | tf_op jit(solution)/shard_map/ppermute | solution.py:96
  64.3 1.5 copy-done.2
  65.8 1.9 fusion.18
  67.7 2.2 copy-done.8
  69.9 1.6 convolution_convert_fusion.4
  71.5 3.2 reshape.301
  74.6 4.7 copy.216
  79.4 4.8 copy.187
  84.2 4.5 fusion.54
  88.7 3.2 reshape.302
  91.9 9.4 %bitcast_subtract_fusion = (f32[16,4,128,64]{3,0,1,2:T(8,128)}, f32[16,4,128,64]{3,0,1,2:T(8,128)}) fusion(f32[16,128,4,64]{3,2,1,0:T(4,128)} %reshape.302), kind=kOutput, calls=%fused_computation.42 | output fusion | flops 67108864 | bytes 6291456 | tf_op jit(solution)/shard_map/jit(cumsum)/reduce_window_sum | solution.py:33
  101.3 4.8 copy.196
  107.2 3.9 convolution_convert_fusion.3
  112.1 3.2 reshape.303
  115.3 3.5 copy.194
  118.8 5.7 %convolution_convert_fusion.2 = bf16[2048,256]{1,0:T(8,128)(2,1)} fusion(bf16[2048,1152]{1,0:T(8,128)(2,1)} %bitcast.152, bf16[1152,256]{1,0:T(8,128)(2,1)} %param.19), kind=kOutput, calls=%fused_computation.66 | convolution fusion | flops 1208483840 | bytes 6356992 | tf_op jit(solution)/shard_map/dot_general | solution.py:110
  124.5 2.3 copy.197
  126.8 1.5 copy.223
  128.3 22.3 %fusion.1 = f32[16,4,8,16,128]{4,3,2,1,0:T(8,128)S(1)} fusion(f32[16,4,128,64]{2,3,1,0:T(8,128)} %copy.196, f32[16,4,8,64]{3,2,1,0:T(8,128)S(1)} %copy.191, f32[16,4,128,64]{2,3,1,0:T(8,128)S(1)} %bitcast.135, pred[8,128]{1,0:T(8,128)(4,1)S(1)} %iota_compare_fusion.1, f32[16,4,8,16,64]{4,3,2,1,0:T(8,128)} %bitcast.161, f32[16,4,8,16,64]{4,0,1,3,2:T(8,128)} %bitcast.147), kind=kOutput, calls=%fused_computation.1 | convolution fusion | flops 818937856 | bytes 12715008 | tf_op jit(solution)/shard_map/nhbqc,nhbsc->nhbqs/dot_general | solution.py:46
  150.6 3.9 fusion.44
  154.5 3.2 copy.200
  157.8 2.9 fusion.57
  161.6 1.7 subtract_multiply_fusion.1
  163.3 2.3 copy.201
  166.9 6.7 %all-to-all-start.3 = ((bf16[1,16,128,256]{3,1,0,2:T(8,128)(2,1)}), bf16[1,16,128,256]{3,1,0,2:T(8,128)(2,1)}, u32[]{:S(2)}, u32[]{:S(2)}) async-start(bf16[1,16,128,256]{3,1,0,2:T(8,128)(2,1)} %multiply_convert_fusion.1), calls=%async_computation.3 | async-start | bytes 2097152 | tf_op jit(solution)/shard_map/all_to_all | solution.py:139
  173.7 2.9 copy.173
  176.5 22.5 %all-to-all-done.3 = bf16[1,16,128,256]{3,1,0,2:T(8,128)(2,1)} async-done(((bf16[1,16,128,256]{3,1,0,2:T(8,128)(2,1)}), bf16[1,16,128,256]{3,1,0,2:T(8,128)(2,1)}, u32[]{:S(2)}, u32[]{:S(2)}) %all-to-all-start.3) | async-done | bytes 1048608 | tf_op jit(solution)/shard_map/all_to_all | solution.py:139
  199.0 4.2 all-to-all-start.1
  203.3 1.6 copy.180
  204.8 23.8 %all-to-all-done.1 = bf16[1,16,128,256]{3,1,0,2:T(8,128)(2,1)} async-done(((bf16[1,16,128,256]{3,1,0,2:T(8,128)(2,1)}), bf16[1,16,128,256]{3,1,0,2:T(8,128)(2,1)}, u32[]{:S(2)}, u32[]{:S(2)}) %all-to-all-start.1) | async-done | bytes 1048608 | tf_op jit(solution)/shard_map/all_to_all | solution.py:138
  228.7 3.6 all-to-all-start.2
  232.3 1.6 copy.168
  233.8 24.2 %all-to-all-done.2 = bf16[1,16,128,256]{3,1,0,2:T(8,128)(2,1)S(1)} async-done(((bf16[1,16,128,256]{3,1,0,2:T(8,128)(2,1)}), bf16[1,16,128,256]{3,1,0,2:T(8,128)(2,1)S(1)}, u32[]{:S(2)}, u32[]{:S(2)}) %all-to-all-start.2) | async-done | bytes 1048608 | tf_op jit(solution)/shard_map/all_to_all | solution.py:137
  258.0 4.3 all-to-all-start
  262.3 1.6 copy.202
  264.0 1.7 copy.204
  265.7 1.6 copy.174
  267.5 1.5 copy.175
  269.0 2.0 copy.176
  271.0 4.6 copy.177
  275.6 7.5 %bitcast_subtract_fusion.1 = (f32[16,4,128,64]{3,0,1,2:T(8,128)}, f32[16,4,128,64]{3,0,1,2:T(8,128)}) fusion(f32[16,128,4,64]{3,0,2,1:T(8,128)} %copy.177), kind=kOutput, calls=%fused_computation.45 | output fusion | flops 67108864 | bytes 6291456 | tf_op jit(solution)/shard_map/jit(cumsum)/reduce_window_sum | solution.py:33
  283.1 4.8 copy.185
  289.9 1.9 copy.183
  291.8 1.6 copy.169
  293.6 1.5 copy.170
  295.1 2.0 copy.171
  297.1 2.7 copy.172
  299.8 22.4 %fusion.6 = f32[16,4,8,16,128]{4,3,2,1,0:T(8,128)S(1)} fusion(f32[16,4,128,64]{2,3,1,0:T(8,128)} %copy.185, f32[16,4,8,64]{3,2,1,0:T(8,128)S(1)} %copy.178, f32[16,4,128,64]{2,3,1,0:T(8,128)} %bitcast.140, pred[8,128]{1,0:T(8,128)(4,1)S(1)} %iota_compare_fusion.1, f32[16,4,8,16,64]{4,3,2,1,0:T(8,128)} %bitcast.160, f32[16,4,8,16,64]{4,0,1,3,2:T(8,128)} %bitcast.145), kind=kOutput, calls=%fused_computation.6 | convolution fusion | flops 818937856 | bytes 12715008 | tf_op jit(solution)/shard_map/nhbqc,nhbsc->nhbqs/dot_general | solution.py:46
  322.1 3.8 fusion.46
  325.9 4.2 copy.205
  330.1 3.2 fusion.80
  334.3 2.0 copy.210
  336.4 1.9 fusion.68
  338.3 30.6 %all_to_all.69 = bf16[1,128,16,256]{3,2,0,1:T(8,128)(2,1)S(1)} all-to-all(bf16[1,128,16,256]{3,2,0,1:T(8,128)(2,1)S(1)} %fusion.68), channel_id=1, replica_groups=mesh['seq'=8,'mp'=4] {'seq'}, dimensions={1} | all-to-all | bytes 2097152 | tf_op jit(solution)/shard_map/all_to_all | solution.py:160
  368.9 3.7 convolution_convert_fusion.1
  373.8 91.0 %all-reduce.2.cloned.1.call-done = bf16[1,16,128,1152]{3,2,1,0:T(8,128)(2,1)} async-done(((bf16[1,16,128,1152]{3,2,1,0:T(8,128)(2,1)}), bf16[1,16,128,1152]{3,2,1,0:T(8,128)(2,1)}) %all-reduce.2.cloned.1.call-update) | async-done | bytes 4718608 | tf_op jit(solution)/shard_map/psum | solution.py:168
  464.8 5.3 convert_reduce_fusion.1
  472.2 3.2 fusion.21
  475.5 8.2 %all-gather.3.cloned.1.call-done = bf16[1152,1152]{1,0:T(8,128)(2,1)} async-done(((bf16[144,1152]{1,0:T(8,128)(2,1)}), bf16[1152,1152]{1,0:T(8,128)(2,1)}) %all-gather.3.cloned.1.call-update) | async-done | bytes 2654224 | tf_op jit(solution)/shard_map/all_gather | solution.py:177
  483.7 18.4 %convolution_convert_fusion = bf16[2048,1152]{1,0:T(8,128)(2,1)} fusion(bf16[1152,1152]{0,1:T(8,128)(2,1)} %all-gather.5.cloned.1.call-done, bf16[2048,1152]{1,0:T(8,128)(2,1)} %bitcast.153, bf16[1152,1152]{1,0:T(8,128)(2,1)} %all-gather.3.cloned.1.call-done), kind=kOutput, calls=%fused_computation.40 | convolution fusion | flops 10881073152 | bytes 14745600 | tf_op jit(solution)/shard_map/dot_general | solution.py:182
  502.1 46.6 %reduce-scatter.2.cloned.1.call-done = bf16[1,16,32,1152]{3,2,1,0:T(8,128)(2,1)} async-done(((bf16[1,16,128,1152]{3,2,1,0:T(8,128)(2,1)}), bf16[1,16,32,1152]{3,2,1,0:T(8,128)(2,1)}) %reduce-scatter.2.cloned.1.call-update) | async-done | bytes 1179664 | tf_op jit(solution)/shard_map/reduce_scatter | solution.py:189
  548.7 2.9 add_convert_fusion
  (104 shorter events, 21.3 us)
Async XLA Ops:
  7.4 361.6 %copy-start = (bf16[256,1152]{1,0:T(8,128)(2,1)S(1)}, bf16[256,1152]{1,0:T(8,128)(2,1)}, u32[]{:S(2)}) copy-start(bf16[256,1152]{1,0:T(8,128)(2,1)} %param.26) | copy-start | bytes 1769476
  7.4 51.3 %copy-start.7 = (bf16[1,16,32,1152]{3,2,1,0:T(8,128)(2,1)S(1)}, bf16[1,16,32,1152]{3,2,1,0:T(8,128)(2,1)}, u32[]{:S(2)}) copy-start(bf16[1,16,32,1152]{3,2,1,0:T(8,128)(2,1)} %param.15) | copy-start | bytes 3538948
  7.4 16.5 %collective-permute-start = (bf16[1,16,32,1152]{3,2,1,0:T(8,128)(2,1)}, bf16[1,16,32,1152]{3,2,1,0:T(8,128)(2,1)S(1)}, u32[]{:S(2)}, u32[]{:S(2)}) collective-permute-start(bf16[1,16,32,1152]{3,2,1,0:T(8,128)(2,1)} %param.15), channel_id=1, source_target_pairs={{0,1},{1,2},{2,3},{3,0},{4,5},{5,6},{6,7},{7,4},{8,9},{9,10},{10,1... | collective-permute-start | bytes 3538952 | tf_op jit(solution)/shard_map/ppermute | solution.py:96
  23.9 15.7 %collective-permute-start.1 = (bf16[1,16,32,1152]{3,2,1,0:T(8,128)(2,1)S(1)}, bf16[1,16,32,1152]{3,2,1,0:T(8,128)(2,1)}, u32[]{:S(2)}, u32[]{:S(2)}) collective-permute-start(bf16[1,16,32,1152]{3,2,1,0:T(8,128)(2,1)S(1)} %collective-permute-done), channel_id=1, source_target_pairs={{0,1},{1,2},{2,3},{3,0},{4,5},{5,6},{6,7},{7,4},{8,9},{9,10},{10,1... | collective-permute-start | bytes 3538952 | tf_op jit(solution)/shard_map/ppermute | solution.py:96
  39.6 15.9 %collective-permute-start.2 = (bf16[1,16,32,1152]{3,2,1,0:T(8,128)(2,1)}, bf16[1,16,32,1152]{3,2,1,0:T(8,128)(2,1)}, u32[]{:S(2)}, u32[]{:S(2)}) collective-permute-start(bf16[1,16,32,1152]{3,2,1,0:T(8,128)(2,1)} %collective-permute-done.1), channel_id=1, source_target_pairs={{0,1},{1,2},{2,3},{3,0},{4,5},{5,6},{6,7},{7,4},{8,9},{9,10},{10,1... | collective-permute-start | bytes 3538952 | tf_op jit(solution)/shard_map/ppermute | solution.py:96
  62.1 3.6 copy-start.2
  62.1 3.6 copy-start.16
  65.8 4.1 copy-start.20
  67.7 2.2 copy-start.8
  71.5 7.9 %copy-start.9 = (bf16[2048,256]{1,0:T(8,128)(2,1)}, bf16[2048,256]{1,0:T(8,128)(2,1)S(1)}, u32[]{:S(2)}) copy-start(bf16[2048,256]{1,0:T(8,128)(2,1)S(1)} %convolution_convert_fusion.4) | copy-start | bytes 3145732
  79.4 4.8 copy-start.22
  79.4 4.8 copy-start.23
  79.4 4.8 copy-start.24
  88.7 12.6 %copy-start.11 = (bf16[2048,256]{1,0:T(8,128)(2,1)}, bf16[2048,256]{1,0:T(8,128)(2,1)S(1)}, u32[]{:S(2)}) copy-start(bf16[2048,256]{1,0:T(8,128)(2,1)S(1)} %fusion.54) | copy-start | bytes 3145732
  101.3 5.9 %copy-start.21 = (bf16[1152,256]{1,0:T(8,128)(2,1)S(1)}, bf16[1152,256]{1,0:T(8,128)(2,1)}, u32[]{:S(2)}) copy-start(bf16[1152,256]{1,0:T(8,128)(2,1)} %param.18) | copy-start | bytes 1769476
  111.1 1.0 copy-start.12
  118.7 9.5 %copy-start.6 = (f32[16,128,4,64]{1,3,2,0:T(8,128)}, f32[16,128,4,64]{1,3,2,0:T(8,128)S(1)}, u32[]{:S(2)}) copy-start(f32[16,128,4,64]{1,3,2,0:T(8,128)S(1)} %copy.194) | copy-start | bytes 6291460
  128.2 22.4 %copy-start.3 = (bf16[32,8,16,128]{3,2,1,0:T(8,128)(2,1)}, bf16[32,8,16,128]{3,2,1,0:T(8,128)(2,1)S(1)}, u32[]{:S(2)}) copy-start(bf16[32,8,16,128]{3,2,1,0:T(8,128)(2,1)S(1)} %copy.223) | copy-start | bytes 3145732
  157.8 2.9 copy-start.4
  161.6 4.1 copy-start.18
  166.9 36.4 %copy-start.13 = (bf16[2048,256]{1,0:T(8,128)(2,1)S(1)}, bf16[2048,256]{1,0:T(8,128)(2,1)}, u32[]{:S(2)}) copy-start(bf16[2048,256]{1,0:T(8,128)(2,1)} %copy-done.12) | copy-start | bytes 3145732
  166.9 32.1 %all-to-all-start.3 = ((bf16[1,16,128,256]{3,1,0,2:T(8,128)(2,1)}), bf16[1,16,128,256]{3,1,0,2:T(8,128)(2,1)}, u32[]{:S(2)}, u32[]{:S(2)}) async-start(bf16[1,16,128,256]{3,1,0,2:T(8,128)(2,1)} %multiply_convert_fusion.1), calls=%async_computation.3 | async-start | bytes 2097152 | tf_op jit(solution)/shard_map/all_to_all | solution.py:139
  173.7 58.6 %copy-start.10 = (bf16[2048,256]{1,0:T(8,128)(2,1)S(1)}, bf16[2048,256]{1,0:T(8,128)(2,1)}, u32[]{:S(2)}) copy-start(bf16[2048,256]{1,0:T(8,128)(2,1)} %copy-done.9) | copy-start | bytes 3145732
  199.0 29.6 %all-to-all-start.1 = ((bf16[1,16,128,256]{3,1,0,2:T(8,128)(2,1)}), bf16[1,16,128,256]{3,1,0,2:T(8,128)(2,1)}, u32[]{:S(2)}, u32[]{:S(2)}) async-start(bf16[1,16,128,256]{3,1,0,2:T(8,128)(2,1)} %copy.173), calls=%async_computation.1 | async-start | bytes 2097152 | tf_op jit(solution)/shard_map/all_to_all | solution.py:138
  228.7 29.3 %all-to-all-start.2 = ((bf16[1,16,128,256]{3,1,0,2:T(8,128)(2,1)}), bf16[1,16,128,256]{3,1,0,2:T(8,128)(2,1)S(1)}, u32[]{:S(2)}, u32[]{:S(2)}) async-start(bf16[1,16,128,256]{3,1,0,2:T(8,128)(2,1)} %copy.180), calls=%async_computation.2 | async-start | bytes 2097152 | tf_op jit(solution)/shard_map/all_to_all | solution.py:137
  258.0 7.7 %copy-start.14 = (bf16[1,16,128,256]{3,1,0,2:T(8,128)(2,1)}, bf16[1,16,128,256]{3,1,0,2:T(8,128)(2,1)S(1)}, u32[]{:S(2)}) copy-start(bf16[1,16,128,256]{3,1,0,2:T(8,128)(2,1)S(1)} %all-to-all-done.2) | copy-start | bytes 3145732
  258.0 33.8 %all-to-all-start = ((bf16[1,16,128,256]{3,1,0,2:T(8,128)(2,1)}), bf16[1,16,128,256]{3,1,0,2:T(8,128)(2,1)}, u32[]{:S(2)}, u32[]{:S(2)}) async-start(bf16[1,16,128,256]{3,1,0,2:T(8,128)(2,1)} %copy.168), calls=%async_computation | async-start | bytes 2097152 | tf_op jit(solution)/shard_map/all_to_all | solution.py:136
  262.3 202.6 %all-reduce.2.cloned.1.call-start = ((), (), s32[]{:S(2)}) async-start(), calls=%async_computation.6 | async-start | bytes 9437184 | tf_op jit(solution)/shard_map/psum | solution.py:168
  283.1 6.0 %copy-start.15 = (bf16[1,16,128,256]{3,1,0,2:T(8,128)(2,1)S(1)}, bf16[1,16,128,256]{3,1,0,2:T(8,128)(2,1)}, u32[]{:S(2)}) copy-start(bf16[1,16,128,256]{3,1,0,2:T(8,128)(2,1)} %copy-done.14) | copy-start | bytes 3145732
  299.8 22.4 %copy-start.5 = (bf16[1,16,128,256]{2,3,1,0:T(8,128)(2,1)S(1)}, bf16[1,16,128,256]{2,3,1,0:T(8,128)(2,1)}, u32[]{:S(2)}) copy-start(bf16[1,16,128,256]{2,3,1,0:T(8,128)(2,1)} %copy.204) | copy-start | bytes 3145732
  333.9 2.5 copy-start.19
  372.6 102.8 %all-gather.5.cloned.1.call-start = ((), (), s32[]{:S(2)}) async-start(), calls=%async_computation.8 | async-start | bytes 2985984 | tf_op jit(solution)/shard_map/all_gather | solution.py:184
  373.2 110.5 %all-gather.3.cloned.1.call-start = ((), (), s32[]{:S(2)}) async-start(), calls=%async_computation.7 | async-start | bytes 2985984 | tf_op jit(solution)/shard_map/all_gather | solution.py:177
  373.8 174.9 %reduce-scatter.2.cloned.1.call-start = ((), (), s32[]{:S(2)}) async-start(), calls=%async_computation.9 | async-start | bytes 5898240 | tf_op jit(solution)/shard_map/reduce_scatter | solution.py:189
  470.1 2.1 copy-start.1
  470.1 2.1 copy-start.17
Sparse Core Ops, SparseCore 0:
  372.7 92.0 all-reduce.1
  502.2 46.4 reduce-scatter.1
Sparse Core Ops, SparseCore 1:
  375.3 52.9 all-gather.4
  430.3 53.4 all-gather.2
